TPU v7x, 32 devices: a whole 2x2x4 slice. The times are simulated.
32 devices in a mesh: parts: 2 (over y), vocab: 4 (over z), mp: 2 (over x), rep: 2 (over core).
Axes of the slice: x: 2, y: 2, z: 4, core: 2. Of those that a mesh axis runs over, the one named last changes fastest.
Arguments:
- resid_base: bfloat16 [128, 4608], P(('parts', 'vocab', 'rep'), 'mp'), parts along dimension 0, may hold values from -60 to 60
- mlp_hidden: bfloat16 [128, 36864], P(('parts', 'vocab', 'rep'), 'mp'), parts along dimension 0, may hold values from -6 to 6
- edit_in: float32 [73728], P(('parts', 'mp')), parts along dimension 0, may hold values from -0.03125 to 0.03125
- edit_out: float32 [9216], P(('parts', 'mp')), parts along dimension 0, may hold values from -6 to 6
- norm_gain: float32 [4608], P('mp'), may hold values from 0.5 to 1.5
- head: bfloat16 [4608, 8192], P(None, ('vocab', 'mp', 'rep')), may hold values from -0.25 to 0.25
- token_ids: int32 [128], P('parts'), parts along dimension 0, may hold values from 0 to 8191
Outputs:
- penalty: float32 [128], P(('parts', 'vocab', 'rep')), parts along dimension 0
- grad_in: float32 [73728], P(('parts', 'mp')), parts along dimension 0
- grad_out: float32 [9216], P(('parts', 'mp')), parts along dimension 0
There are 2 independent parts, one for each index of `parts`. A program takes and returns all parts, laid end to end along the dimension named above; an argument that names none is the same for every part. Nothing has to cross between parts.
All inputs are finite; a program needn't handle non-finite values.
Results may differ from a plain program's by a relative error of at most 0.011.
Values may be sent and summed in bfloat16 or wider, within the bound.
No kernel may reach another device: no remote copies, remote signals or barrier semaphores. Data moves between devices by JAX's collectives and lax.ppermute only.
A program may use at most 64 MiB of HBM per device.

v0:
```python
import jax
import jax.numpy as jnp
from jax import lax
from jax.sharding import PartitionSpec as P

D = 4608
softcap = 30.0
epsilon = 1e-06


def local(resid_base, mlp_hidden, edit_in, edit_out, norm_gain, head, token_ids):
    tok_rows = resid_base.shape[0]
    feat_cols = resid_base.shape[1]
    voc_cols = head.shape[1]
    hidden_f = mlp_hidden.astype(jnp.float32)
    base_f = resid_base.astype(jnp.float32)
    mix_part = jnp.sum(hidden_f * edit_in[None, :], axis=1)
    mix_scale, square_base, base_along, out_square = lax.psum(
        (
            mix_part,
            jnp.sum(base_f * base_f, axis=1),
            jnp.sum(base_f * edit_out[None, :], axis=1),
            jnp.sum(edit_out * edit_out),
        ),
        "mp",
    )
    resid = base_f + mix_scale[:, None] * edit_out[None, :]
    square_edit = square_base + 2.0 * mix_scale * base_along + mix_scale * mix_scale * out_square
    along = base_along + mix_scale * out_square
    edit_scale = lax.rsqrt(square_edit / D + epsilon)
    base_scale = lax.rsqrt(square_base / D + epsilon)
    x_edit = (resid * edit_scale[:, None] * norm_gain[None, :]).astype(jnp.bfloat16)
    x_base = (base_f * base_scale[:, None] * norm_gain[None, :]).astype(jnp.bfloat16)
    stacked = jnp.stack([x_edit, x_base], axis=0)
    direction = lax.all_gather(edit_out * norm_gain, "mp", axis=0, tiled=True)
    weights_all = lax.all_gather(mix_scale * edit_scale, ("vocab", "rep"), axis=0, tiled=True)
    full_cols = lax.all_gather(stacked, "mp", axis=2, tiled=True)
    logits_pre = jnp.einsum(
        "ktd,dv->ktv",
        lax.all_gather(full_cols, ("vocab", "rep"), axis=1, tiled=True),
        head,
        preferred_element_type=jnp.float32,
    )
    capped = softcap * jnp.tanh(logits_pre / softcap)
    totals = lax.psum(jnp.sum(jnp.exp(capped), axis=2), ("vocab", "mp", "rep"))
    log_totals = jnp.log(totals)
    probs = jnp.exp(capped - log_totals[:, :, None])
    z_edit = capped[0]
    z_base = capped[1]
    first_col = lax.axis_index(("vocab", "mp", "rep")) * voc_cols
    columns = first_col + jnp.arange(voc_cols, dtype=jnp.int32)
    onehot = (token_ids[:, None] == columns[None, :]).astype(jnp.float32)
    diff = z_base - z_edit
    kl_part = jnp.sum(probs[1] * diff, axis=1)
    gap_part = jnp.sum(onehot * diff, axis=1)
    dy_rows = ((2.0 * probs[0] - probs[1] - onehot) * (1.0 - (z_edit / softcap) ** 2)).astype(
        jnp.bfloat16
    )
    dx_part = lax.dot_general(
        dy_rows, head, (((1,), (1,)), ((), ())), preferred_element_type=jnp.float32
    )
    align_part = jnp.sum(logits_pre[0] * dy_rows.astype(jnp.float32), axis=1)
    proj_part = jnp.dot(dx_part, direction, precision=lax.Precision.HIGHEST)
    weighted_part = jnp.dot(weights_all, dx_part, precision=lax.Precision.HIGHEST)
    kl_all, gap_all, proj_all, align_all, weighted_all = lax.psum(
        (kl_part, gap_part, proj_part, align_part, weighted_part), ("vocab", "mp", "rep")
    )
    tok_start = lax.axis_index(("vocab", "rep")) * tok_rows
    feat_start = lax.axis_index("mp") * feat_cols
    kl_own = lax.dynamic_slice_in_dim(kl_all, tok_start, tok_rows, 0)
    gap_own = lax.dynamic_slice_in_dim(gap_all, tok_start, tok_rows, 0)
    proj_own = lax.dynamic_slice_in_dim(proj_all, tok_start, tok_rows, 0)
    align_own = lax.dynamic_slice_in_dim(align_all, tok_start, tok_rows, 0)
    lse_own = lax.dynamic_slice_in_dim(log_totals, tok_start, tok_rows, 1)
    penalty = kl_own + gap_own + 2.0 * (lse_own[0] - lse_own[1])
    normed = resid * edit_scale[:, None]
    shrink = edit_scale * align_own / D
    coeff = edit_scale * proj_own - shrink * (edit_scale * along)
    second_part = jnp.sum((mix_scale * shrink)[:, None] * normed, axis=0)
    grad_in_part = jnp.sum(coeff[:, None] * hidden_f, axis=0)
    second_sum, grad_in = lax.psum((second_part, grad_in_part), ("vocab", "rep"))
    weighted_own = lax.dynamic_slice_in_dim(weighted_all, feat_start, feat_cols, 0)
    grad_out = norm_gain * weighted_own - second_sum
    return (penalty, grad_in, grad_out)


def solution(mesh):
    in_specs = (
        P(("parts", "vocab", "rep"), "mp"),
        P(("parts", "vocab", "rep"), "mp"),
        P(("parts", "mp")),
        P(("parts", "mp")),
        P("mp"),
        P(None, ("vocab", "mp", "rep")),
        P("parts"),
    )
    out_specs = (P(("parts", "vocab", "rep")), P(("parts", "mp")), P(("parts", "mp")))
    return jax.shard_map(local, mesh=mesh, in_specs=in_specs, out_specs=out_specs, check_vma=False)
```

profile of v0, /device:TPU:8, one launch (start us, length us, event | category | flops | bytes accessed | tf_op | source)
XLA Modules:
  0.0 234.1 jit_solution(15880379331970252911)
XLA Ops:
  7.2 0.0 all-gather.3.cloned.1.call-start
  7.2 1.3 fusion.23
  8.6 0.9 fusion.15
  9.5 1.2 fusion.2
  10.7 1.2 dynamic-slice
  12.6 5.6 %all-reduce.2 = (f32[8]{0:T(128)S(1)}, f32[8]{0:T(128)S(1)}, f32[8]{0:T(128)S(1)}, f32[]{:T(128)}) all-reduce(f32[8]{0:T(128)S(1)} %get-tuple-element.6, f32[8]{0:T(128)S(1)} %fusion.2, f32[8]{0:T(128)S(1)} %get-tuple-element.5, f32[]{:T(128)} %get-tuple-element.26), channel_id=1, replica_groups=mesh['parts'=2,'vocab'=4,'mp'=2,'rep'=2] {'mp'}, use_global_device_ids=true, to_apply=%region_3.0 | all-reduce | flops 25 | bytes 200 | tf_op jit(solution)/shard_map/psum | solution.py:18
  18.2 0.7 multiply_dynamic-update-slice_fusion
  19.0 0.9 fusion.18
  19.9 5.1 %all_gather.12 = bf16[2,8,4608]{2,1,0:T(8,128)(2,1)} all-gather(bf16[2,8,2304]{2,1,0:T(8,128)(2,1)S(1)} %pad_maximum_fusion), channel_id=1, replica_groups=mesh['parts'=2,'vocab'=4,'mp'=2,'rep'=2] {'mp'}, dimensions={2}, use_global_device_ids=true | all-gather | bytes 221184 | tf_op jit(solution)/shard_map/all_gather | solution.py:37
  25.0 0.0 all-gather.3.cloned.1.call-update
  25.0 0.0 all-reduce.5.cloned.1.call-start
  25.1 10.7 %all-reduce = f32[64]{0:T(128)S(1)} all-reduce(f32[64]{0:T(128)S(1)} %get-tuple-element.15), channel_id=1, replica_groups=mesh['parts'=2,'vocab'=4,'mp'=2,'rep'=2] {'vocab','rep'}, use_global_device_ids=true, to_apply=%add | all-reduce | flops 64 | bytes 512
  35.8 4.4 %all-gather = f32[2,1,2304]{2,1,0:T(1,128)S(1)} all-gather(f32[1,1,2304]{2,1,0:T(1,128)S(1)} %reshape.34), channel_id=1, replica_groups=mesh['parts'=2,'vocab'=4,'mp'=2,'rep'=2] {'mp'}, dimensions={0}, use_global_device_ids=true | all-gather | bytes 27648 | tf_op jit(solution)/shard_map/all_gather | solution.py:35
  40.2 0.0 copy-start.4
  40.2 9.0 %all-gather.3.cloned.1.call-done = bf16[2,64,4608]{2,1,0:T(8,128)(2,1)} async-done(((bf16[2,8,4608]{2,1,0:T(8,128)(2,1)}), bf16[2,64,4608]{2,1,0:T(8,128)(2,1)}) %all-gather.3.cloned.1.call-update) | async-done | bytes 1179664 | tf_op jit(solution)/shard_map/all_gather | solution.py:40
  49.2 3.6 %exponential_reduce_fusion = (f32[2,64]{1,0:T(2,128)S(1)}, f32[2,64,512]{2,1,0:T(8,128)S(1)}) fusion(bf16[2,64,4608]{2,1,0:T(8,128)(2,1)} %all-gather.3.cloned.1.call-done, bf16[4608,512]{1,0:T(8,128)(2,1)} %param.12), kind=kOutput, calls=%fused_computation.9 | convolution fusion | flops 604176256 | bytes 6160896 | tf_op jit(solution)/shard_map/ktd,dv->ktv/dot_general | solution.py:38
  52.8 24.3 %psum.88 = f32[2,64]{1,0:T(2,128)S(1)} all-reduce(f32[2,64]{1,0:T(2,128)S(1)} %get-tuple-element.30), channel_id=1, replica_groups=mesh['parts'=2,'vocab'=4,'mp'=2,'rep'=2] {'vocab','mp','rep'}, use_global_device_ids=true, to_apply=%region_9.0 | all-reduce | flops 128 | bytes 1024 | tf_op jit(solution)/shard_map/psum | solution.py:45
  77.1 0.1 subtract_exponential_fusion
  77.2 0.0 copy-done.4
  77.2 0.2 fusion.9
  77.4 3.9 %fusion.24 = f32[64,4608]{1,0:T(8,128)S(1)} fusion(bf16[64,512]{1,0:T(8,128)(2,1)S(1)} %get-tuple-element.18, bf16[4608,512]{1,0:T(8,128)(2,1)} %param.12), kind=kOutput, calls=%fused_computation.54 | convolution fusion | flops 301989888 | bytes 5963776 | tf_op jit(solution)/shard_map/dot_general | solution.py:59
  81.3 0.0 copy-start.1
  81.3 0.0 copy-start.2
  81.3 0.0 copy-start
  81.3 0.7 convolution_reduce_fusion
  82.0 0.0 copy-start.3
  82.0 1.0 convolution_bitcast_fusion
  83.1 0.1 constant_dynamic-slice_fusion
  83.1 57.7 %all-reduce.1 = (f32[64]{0:T(128)S(1)}, f32[64]{0:T(128)S(1)}, f32[64]{0:T(128)S(1)}, f32[4608]{0:T(1024)S(1)}) all-reduce(f32[64]{0:T(128)S(1)} %add.92, f32[64]{0:T(128)S(1)} %convolution_bitcast_fusion, f32[64]{0:T(128)S(1)} %get-tuple-element.17, ...), channel_id=1, replica_groups=mesh['parts'=2,'vocab'=4,'mp'=2,'rep'=2] {'vocab','mp','rep'}, use_global_device_ids=true, to_apply=%region_11.0 | all-reduce | flops 4800 | bytes 38400 | tf_op jit(solution)/shard_map/psum | solution.py:65
  140.8 0.7 fusion.21
  141.5 0.0 copy-done.1
  141.5 0.0 copy-done.2
  141.5 0.1 multiply_reduce_fusion.1
  141.6 30.3 %psum.95 = f32[2304]{0:T(1024)S(1)} all-reduce(f32[2304]{0:T(1024)S(1)} %multiply_reduce_fusion.1), channel_id=1, replica_groups=mesh['parts'=2,'vocab'=4,'mp'=2,'rep'=2] {'vocab','rep'}, use_global_device_ids=true, to_apply=%region_21.0 | all-reduce | flops 2304 | bytes 18432 | tf_op jit(solution)/shard_map/psum | solution.py:81
  171.9 0.0 copy-done
  171.9 1.0 fusion.3
  172.9 0.0 all-reduce.5.cloned.1.call-update
  172.9 0.0 copy-done.3
  173.0 0.7 multiply_subtract_fusion
  173.6 0.6 bitcast_add_fusion
  174.2 51.5 %all-reduce.5.cloned.1.call-done = f32[18432]{0:T(1024)} async-done(((f32[18432]{0:T(1024)}), f32[18432]{0:T(1024)}) %all-reduce.5.cloned.1.call-update) | async-done | bytes 73744 | tf_op jit(solution)/shard_map/psum | solution.py:81
  225.7 1.5 copy.12
  (6 shorter events, 0.0 us)
Async XLA Ops:
  7.2 42.0 %all-gather.3.cloned.1.call-start = ((), (), s32[]{:S(2)}) async-start(), calls=%async_computation | async-start | bytes 1327104 | tf_op jit(solution)/shard_map/all_gather | solution.py:40
  25.0 200.7 %all-reduce.5.cloned.1.call-start = ((), (), s32[]{:S(2)}) async-start(), calls=%async_computation.1 | async-start | bytes 147456 | tf_op jit(solution)/shard_map/psum | solution.py:81
  40.2 37.0 %copy-start.4 = (s32[64]{0:T(128)S(1)}, s32[64]{0:T(128)}, u32[]{:S(2)}) copy-start(s32[64]{0:T(128)} %param.13) | copy-start | bytes 772
  81.3 60.2 %copy-start.1 = (bf16[8,2304]{1,0:T(8,128)(2,1)S(1)}, bf16[8,2304]{1,0:T(8,128)(2,1)}, u32[]{:S(2)}) copy-start(bf16[8,2304]{1,0:T(8,128)(2,1)} %param.7) | copy-start | bytes 110596
  81.3 60.2 %copy-start.2 = (f32[2304]{0:T(1024)S(1)}, f32[2304]{0:T(1024)}, u32[]{:S(2)}) copy-start(f32[2304]{0:T(1024)} %param.10) | copy-start | bytes 27652
  81.3 90.6 %copy-start = (bf16[8,18432]{1,0:T(8,128)(2,1)S(1)}, bf16[8,18432]{1,0:T(8,128)(2,1)}, u32[]{:S(2)}) copy-start(bf16[8,18432]{1,0:T(8,128)(2,1)} %param.8) | copy-start | bytes 884740
  82.0 90.9 %copy-start.3 = (f32[2304]{0:T(1024)S(1)}, f32[2304]{0:T(1024)}, u32[]{:S(2)}) copy-start(f32[2304]{0:T(1024)} %param.11) | copy-start | bytes 27652
Sparse Core Ops, SparseCore 0:
  25.1 24.0 all-gather.2
  173.1 52.6 all-reduce.4
where the time goes:
time: 235 us; the launch traced here: 234 us
  blocking collectives  138 us (59%)
  waiting for transfers between devices  60.5 us (26%)
  between operations  14.8 us (6%)
  matrix products  9.18 us (4%)
  other arithmetic  8.58 us (4%)
  local copies, waits for them, and re-layouts  2.88 us (1%)
    psum x1, blocking collectives, local(): lax.psum((kl_part, gap_part, proj_part, align_part, weighted_part), ('voc...  57.7 us
    psum x1, waiting for transfers between devices, local(): lax.psum((second_part, grad_in_part), ('vocab', 'rep'))  51.5 us
    psum x1, blocking collectives, local(): lax.psum((second_part, grad_in_part), ('vocab', 'rep'))  30.3 us
    psum x1, blocking collectives, local(): totals = lax.psum(jnp.sum(jnp.exp(capped), axis=2), ('vocab', 'mp', 'rep'))  24.3 us
    unnamed x1, blocking collectives  10.7 us
    all_gather x1, waiting for transfers between devices, local(): lax.all_gather(full_cols, ('vocab', 'rep'), axis=1, tiled=True)  9 us
    psum x1, blocking collectives, local(): lax.psum((mix_part, jnp.sum(base_f * base_f, axis=1), jnp.sum(base_f * ed...  5.58 us
    all_gather x1, blocking collectives, local(): full_cols = lax.all_gather(stacked, 'mp', axis=2, tiled=True)  5.14 us
  transfers between devices with their start and end apart: 2, of which 2 were waited for; matrix products, arithmetic and copies ran while one was open for 1% of the time, Pallas kernels for 0%

commit v1 on v0

--- a/solution.py
+++ b/solution.py
@@ -42,7 +42,7 @@
         preferred_element_type=jnp.float32,
     )
     capped = softcap * jnp.tanh(logits_pre / softcap)
-    totals = lax.psum(jnp.sum(jnp.exp(capped), axis=2), ("vocab", "mp", "rep"))
+    totals = lax.psum(lax.psum(jnp.sum(jnp.exp(capped), axis=2), ("mp", "rep")), "vocab")
     log_totals = jnp.log(totals)
     probs = jnp.exp(capped - log_totals[:, :, None])
     z_edit = capped[0]

time: 235 us -> 220 us (0.936)
  blocking collectives: 138 us -> 123 us
    psum x1 -> x2, blocking collectives: 24.3 us -> 15.6 us  [the longest x1 8.82 us: local(): lax.psum(lax.psum(jnp.sum(jnp.exp(capped), axis=2), ('mp', 'rep')), 'vocab')]
    psum x1, blocking collectives: 57.7 us -> 51.4 us  [local(): lax.psum((kl_part, gap_part, proj_part, align_part, weighted_part), ('voc...]
where the time goes in v1:
time: 220 us; the launch traced here: 219 us
  blocking collectives  123 us (56%)
  waiting for transfers between devices  60.5 us (28%)
  between operations  14.8 us (7%)
  matrix products  9.19 us (4%)
  other arithmetic  8.58 us (4%)
  local copies, waits for them, and re-layouts  2.88 us (1%)
    psum x1, waiting for transfers between devices, local(): lax.psum((second_part, grad_in_part), ('vocab', 'rep'))  51.5 us
    psum x1, blocking collectives, local(): lax.psum((kl_part, gap_part, proj_part, align_part, weighted_part), ('voc...  51.4 us
    psum x1, blocking collectives, local(): lax.psum((second_part, grad_in_part), ('vocab', 'rep'))  30.3 us
    unnamed x1, blocking collectives  10.7 us
    all_gather x1, waiting for transfers between devices, local(): lax.all_gather(full_cols, ('vocab', 'rep'), axis=1, tiled=True)  9 us
    psum x1, blocking collectives, local(): lax.psum(lax.psum(jnp.sum(jnp.exp(capped), axis=2), ('mp', 'rep')), 'vocab')  8.82 us
    psum x1, blocking collectives, local(): lax.psum(jnp.sum(jnp.exp(capped), axis=2), ('mp', 'rep'))  6.81 us
    psum x1, blocking collectives, local(): lax.psum((mix_part, jnp.sum(base_f * base_f, axis=1), jnp.sum(base_f * ed...  5.58 us
  transfers between devices with their start and end apart: 2, of which 2 were waited for; matrix products, arithmetic and copies ran while one was open for 1% of the time, Pallas kernels for 0%

profile of v1, /device:TPU:8, one launch (start us, length us, event | category | flops | bytes accessed | tf_op | source)
XLA Modules:
  0.0 219.2 jit_solution(3868964841620531896)
XLA Ops:
  7.2 0.0 all-gather.3.cloned.1.call-start
  7.2 1.3 fusion.23
  8.6 0.9 fusion.15
  9.5 1.2 fusion.2
  10.7 1.2 dynamic-slice
  12.6 5.6 %all-reduce.2 = (f32[8]{0:T(128)S(1)}, f32[8]{0:T(128)S(1)}, f32[8]{0:T(128)S(1)}, f32[]{:T(128)}) all-reduce(f32[8]{0:T(128)S(1)} %get-tuple-element.6, f32[8]{0:T(128)S(1)} %fusion.2, f32[8]{0:T(128)S(1)} %get-tuple-element.5, f32[]{:T(128)} %get-tuple-element.26), channel_id=1, replica_groups=mesh['parts'=2,'vocab'=4,'mp'=2,'rep'=2] {'mp'}, use_global_device_ids=true, to_apply=%region_3.0 | all-reduce | flops 25 | bytes 200 | tf_op jit(solution)/shard_map/psum | solution.py:18
  18.2 0.7 multiply_dynamic-update-slice_fusion
  19.0 0.9 fusion.18
  19.9 5.1 %all_gather.12 = bf16[2,8,4608]{2,1,0:T(8,128)(2,1)} all-gather(bf16[2,8,2304]{2,1,0:T(8,128)(2,1)S(1)} %pad_maximum_fusion), channel_id=1, replica_groups=mesh['parts'=2,'vocab'=4,'mp'=2,'rep'=2] {'mp'}, dimensions={2}, use_global_device_ids=true | all-gather | bytes 221184 | tf_op jit(solution)/shard_map/all_gather | solution.py:37
  25.0 0.0 all-gather.3.cloned.1.call-update
  25.0 0.0 all-reduce.5.cloned.1.call-start
  25.1 10.7 %all-reduce = f32[64]{0:T(128)S(1)} all-reduce(f32[64]{0:T(128)S(1)} %get-tuple-element.15), channel_id=1, replica_groups=mesh['parts'=2,'vocab'=4,'mp'=2,'rep'=2] {'vocab','rep'}, use_global_device_ids=true, to_apply=%add | all-reduce | flops 64 | bytes 512
  35.8 4.4 %all-gather = f32[2,1,2304]{2,1,0:T(1,128)S(1)} all-gather(f32[1,1,2304]{2,1,0:T(1,128)S(1)} %reshape.34), channel_id=1, replica_groups=mesh['parts'=2,'vocab'=4,'mp'=2,'rep'=2] {'mp'}, dimensions={0}, use_global_device_ids=true | all-gather | bytes 27648 | tf_op jit(solution)/shard_map/all_gather | solution.py:35
  40.2 0.0 copy-start.4
  40.2 9.0 %all-gather.3.cloned.1.call-done = bf16[2,64,4608]{2,1,0:T(8,128)(2,1)} async-done(((bf16[2,8,4608]{2,1,0:T(8,128)(2,1)}), bf16[2,64,4608]{2,1,0:T(8,128)(2,1)}) %all-gather.3.cloned.1.call-update) | async-done | bytes 1179664 | tf_op jit(solution)/shard_map/all_gather | solution.py:40
  49.2 3.6 %exponential_reduce_fusion = (f32[2,64]{1,0:T(2,128)S(1)}, f32[2,64,512]{2,1,0:T(8,128)S(1)}) fusion(bf16[2,64,4608]{2,1,0:T(8,128)(2,1)} %all-gather.3.cloned.1.call-done, bf16[4608,512]{1,0:T(8,128)(2,1)} %param.12), kind=kOutput, calls=%fused_computation.9 | convolution fusion | flops 604176256 | bytes 6160896 | tf_op jit(solution)/shard_map/ktd,dv->ktv/dot_general | solution.py:38
  52.8 6.8 %psum.95 = f32[2,64]{1,0:T(2,128)S(1)} all-reduce(f32[2,64]{1,0:T(2,128)S(1)} %get-tuple-element.30), channel_id=1, replica_groups=mesh['parts'=2,'vocab'=4,'mp'=2,'rep'=2] {'mp','rep'}, use_global_device_ids=true, to_apply=%region_9.0 | all-reduce | flops 128 | bytes 1024 | tf_op jit(solution)/shard_map/psum | solution.py:45
  59.6 8.8 %psum.96 = f32[2,64]{1,0:T(2,128)S(1)} all-reduce(f32[2,64]{1,0:T(2,128)S(1)} %psum.95), channel_id=1, replica_groups=mesh['parts'=2,'vocab'=4,'mp'=2,'rep'=2] {'vocab'}, use_global_device_ids=true, to_apply=%region_10.0 | all-reduce | flops 128 | bytes 1024 | tf_op jit(solution)/shard_map/psum | solution.py:45
  68.4 0.1 subtract_exponential_fusion
  68.6 0.0 copy-done.4
  68.6 0.2 fusion.9
  68.8 3.9 %fusion.24 = f32[64,4608]{1,0:T(8,128)S(1)} fusion(bf16[64,512]{1,0:T(8,128)(2,1)S(1)} %get-tuple-element.18, bf16[4608,512]{1,0:T(8,128)(2,1)} %param.12), kind=kOutput, calls=%fused_computation.54 | convolution fusion | flops 301989888 | bytes 5963776 | tf_op jit(solution)/shard_map/dot_general | solution.py:59
  72.7 0.0 copy-start.1
  72.7 0.0 copy-start.2
  72.7 0.0 copy-start
  72.7 0.7 convolution_reduce_fusion
  73.4 0.0 copy-start.3
  73.4 1.0 convolution_bitcast_fusion
  74.4 0.1 constant_dynamic-slice_fusion
  74.5 51.4 %all-reduce.1 = (f32[64]{0:T(128)S(1)}, f32[64]{0:T(128)S(1)}, f32[64]{0:T(128)S(1)}, f32[4608]{0:T(1024)S(1)}) all-reduce(f32[64]{0:T(128)S(1)} %add.94, f32[64]{0:T(128)S(1)} %convolution_bitcast_fusion, f32[64]{0:T(128)S(1)} %get-tuple-element.17, ...), channel_id=1, replica_groups=mesh['parts'=2,'vocab'=4,'mp'=2,'rep'=2] {'vocab','mp','rep'}, use_global_device_ids=true, to_apply=%region_12.0 | all-reduce | flops 4800 | bytes 38400 | tf_op jit(solution)/shard_map/psum | solution.py:65
  125.9 0.7 fusion.21
  126.6 0.0 copy-done.1
  126.6 0.0 copy-done.2
  126.6 0.1 multiply_reduce_fusion.1
  126.7 30.3 %psum.103 = f32[2304]{0:T(1024)S(1)} all-reduce(f32[2304]{0:T(1024)S(1)} %multiply_reduce_fusion.1), channel_id=1, replica_groups=mesh['parts'=2,'vocab'=4,'mp'=2,'rep'=2] {'vocab','rep'}, use_global_device_ids=true, to_apply=%region_22.0 | all-reduce | flops 2304 | bytes 18432 | tf_op jit(solution)/shard_map/psum | solution.py:81
  157.0 0.0 copy-done
  157.1 1.0 fusion.3
  158.0 0.0 all-reduce.5.cloned.1.call-update
  158.1 0.0 copy-done.3
  158.1 0.7 multiply_subtract_fusion
  158.8 0.6 bitcast_add_fusion
  159.3 51.5 %all-reduce.5.cloned.1.call-done = f32[18432]{0:T(1024)} async-done(((f32[18432]{0:T(1024)}), f32[18432]{0:T(1024)}) %all-reduce.5.cloned.1.call-update) | async-done | bytes 73744 | tf_op jit(solution)/shard_map/psum | solution.py:81
  210.8 1.5 copy.12
  (6 shorter events, 0.0 us)
Async XLA Ops:
  7.2 42.0 %all-gather.3.cloned.1.call-start = ((), (), s32[]{:S(2)}) async-start(), calls=%async_computation | async-start | bytes 1327104 | tf_op jit(solution)/shard_map/all_gather | solution.py:40
  25.0 185.8 %all-reduce.5.cloned.1.call-start = ((), (), s32[]{:S(2)}) async-start(), calls=%async_computation.1 | async-start | bytes 147456 | tf_op jit(solution)/shard_map/psum | solution.py:81
  40.2 28.4 %copy-start.4 = (s32[64]{0:T(128)S(1)}, s32[64]{0:T(128)}, u32[]{:S(2)}) copy-start(s32[64]{0:T(128)} %param.13) | copy-start | bytes 772
  72.7 54.0 %copy-start.1 = (bf16[8,2304]{1,0:T(8,128)(2,1)S(1)}, bf16[8,2304]{1,0:T(8,128)(2,1)}, u32[]{:S(2)}) copy-start(bf16[8,2304]{1,0:T(8,128)(2,1)} %param.7) | copy-start | bytes 110596
  72.7 53.9 %copy-start.2 = (f32[2304]{0:T(1024)S(1)}, f32[2304]{0:T(1024)}, u32[]{:S(2)}) copy-start(f32[2304]{0:T(1024)} %param.10) | copy-start | bytes 27652
  72.7 84.3 %copy-start = (bf16[8,18432]{1,0:T(8,128)(2,1)S(1)}, bf16[8,18432]{1,0:T(8,128)(2,1)}, u32[]{:S(2)}) copy-start(bf16[8,18432]{1,0:T(8,128)(2,1)} %param.8) | copy-start | bytes 884740
  73.4 84.7 %copy-start.3 = (f32[2304]{0:T(1024)S(1)}, f32[2304]{0:T(1024)}, u32[]{:S(2)}) copy-start(f32[2304]{0:T(1024)} %param.11) | copy-start | bytes 27652
Sparse Core Ops, SparseCore 0:
  25.1 24.0 all-gather.2
  158.2 52.5 all-reduce.4
